TPU v7x, 32 devices: a whole 2x2x4 slice. The times are simulated.
32 devices in a mesh: layer: 2 (over y), latent: 8 (over z, x), tok: 2 (over core).
Axes of the slice: x: 2, y: 2, z: 4, core: 2. Of those that a mesh axis runs over, the one named last changes fastest.
Arguments:
- resid: bfloat16 [2, 384, 2304], P('layer', 'tok', 'latent'), may hold values from -6 to 6
- w_enc: bfloat16 [2, 2304, 2048], P('layer', None, 'latent'), may hold values from -0.09375 to 0.09375
- b_enc: float32 [2048], P('latent'), may hold values from -3 to 3
- w_dec: bfloat16 [2, 2048, 2304], P('layer', 'latent'), may hold values from -0.125 to 0.125
- b_dec: bfloat16 [2, 2304], P('layer', 'latent'), may hold values from -3 to 3
Outputs:
- grad_w_enc: bfloat16 [2, 2304, 2048], P('layer', 'tok', 'latent')
- grad_w_dec: bfloat16 [2, 2048, 2304], P('layer', 'latent')
All inputs are finite; a program needn't handle non-finite values.
Results may differ from a plain program's by a relative error of at most 0.023.
Values may be sent and summed in bfloat16 or wider, within the bound.
A program may use at most 64 MiB of HBM per device.

v0:
```python
import jax
import jax.numpy as jnp
from jax import lax
from jax.sharding import PartitionSpec as P

BETA = 4.0


def shards(resid, w_enc, b_enc, w_dec, b_dec):
    decoder = w_dec[0]
    x_full, bias_full = (
        lax.all_gather(resid, "latent", axis=2, tiled=True),
        lax.all_gather(b_dec.reshape(1, 1, -1), "latent", axis=2, tiled=True),
    )
    x_full = x_full[0]
    bias_full = bias_full.reshape(-1).astype(jnp.float32)
    tok_rows = x_full.shape[0]
    tokens = tok_rows * lax.axis_size("tok")
    partial_value = jnp.dot(x_full, w_enc[0], preferred_element_type=jnp.float32)
    pre = lax.psum(partial_value.astype(jnp.bfloat16), "layer").astype(jnp.float32) + b_enc
    act = (jax.nn.softplus(BETA * pre) / BETA).astype(jnp.bfloat16)
    slope = jax.nn.sigmoid(BETA * pre)
    recon = lax.psum(
        jnp.dot(act, decoder, preferred_element_type=jnp.float32).astype(jnp.bfloat16), "latent"
    ).astype(jnp.float32)
    grad_all = (2.0 / tokens * (recon + bias_full - x_full.astype(jnp.float32))).astype(
        jnp.bfloat16
    )
    dec_sum = lax.dot_general(
        act, grad_all, (((0,), (0,)), ((), ())), preferred_element_type=jnp.float32
    )
    rows_grad = lax.dot_general(
        grad_all, decoder, (((1,), (1,)), ((), ())), preferred_element_type=jnp.float32
    )
    act_grad = rows_grad
    dec_sum, act_grad = (dec_sum, act_grad)
    grad_act = lax.psum(act_grad.astype(jnp.bfloat16), "layer").astype(jnp.float32)
    grad_pre = (grad_act * slope).astype(jnp.bfloat16)
    grad_w_dec = lax.psum(dec_sum.astype(jnp.bfloat16), "tok")
    grad_w_enc = lax.psum_scatter(
        lax.dot_general(
            x_full, grad_pre, (((0,), (0,)), ((), ())), preferred_element_type=jnp.float32
        ).astype(jnp.bfloat16),
        "tok",
        scatter_dimension=0,
        tiled=True,
    )
    return (grad_w_enc[None], grad_w_dec[None])


def solution(mesh):
    placed = (
        P("layer", "tok", "latent"),
        P("layer", None, "latent"),
        P("latent"),
        P("layer", "latent", None),
        P("layer", "latent"),
    )
    return jax.shard_map(
        shards,
        mesh=mesh,
        in_specs=placed,
        out_specs=(P("layer", "tok", "latent"), P("layer", "latent", None)),
        check_vma=False,
    )
```

profile of v0, /device:TPU:0, one launch (start us, length us, event | category | flops | bytes accessed | tf_op | source)
XLA Modules:
  0.0 235.1 jit_solution(12181217095717214668)
XLA Ops:
  7.2 0.0 copy-start
  7.2 0.0 all-reduce.6.cloned.1.call-start
  7.2 1.9 copy.8
  9.1 51.7 %all_gather.6 = bf16[1,192,2304]{1,0,2:T(2,128)(2,1)S(1)} all-gather(bf16[1,192,288]{1,0,2:T(2,128)(2,1)} %copy.8), channel_id=1, replica_groups=mesh['layer'=2,'latent'=8,'tok'=2] {'latent'}, dimensions={2}, use_global_device_ids=true | all-gather | bytes 995328 | tf_op jit(solution)/shard_map/all_gather | solution.py:12
  60.8 4.9 %copy.9 = bf16[1,192,2304]{2,1,0:T(8,128)(2,1)} copy(bf16[1,192,2304]{1,0,2:T(2,128)(2,1)S(1)} %all_gather.6) | data formatting | bytes 1769472 | tf_op jit(solution)/shard_map/all_gather | solution.py:12
  65.7 0.0 copy-start.4
  65.7 2.6 %fusion.7 = bf16[192,256]{1,0:T(8,128)(2,1)} fusion(bf16[1,2304,256]{2,1,0:T(8,128)(2,1)} %param.6, bf16[1,192,2304]{2,1,0:T(8,128)(2,1)} %copy.9), kind=kOutput, calls=%fused_computation.11 | convolution fusion | flops 226541568 | bytes 2162688 | tf_op jit(solution)/shard_map/dot_general | solution.py:19
  68.3 0.0 copy-start.5
  68.3 0.0 copy-start.3
  68.3 0.0 copy-start.1
  68.3 0.0 all-reduce.6.cloned.1.call-update
  68.3 0.0 all-reduce.8.cloned.1.call-start
  68.4 20.0 %all-reduce.6.cloned.1.call-done = bf16[192,256]{1,0:T(8,128)(2,1)} async-done(((bf16[192,256]{1,0:T(8,128)(2,1)}), bf16[192,256]{1,0:T(8,128)(2,1)}) %all-reduce.6.cloned.1.call-update) | async-done | bytes 98320 | tf_op jit(solution)/shard_map/psum | solution.py:20
  88.3 0.0 copy-done
  88.3 0.0 copy-done.4
  88.3 2.3 convolution_convert_fusion.2
  90.7 0.0 all-reduce.8.cloned.1.call-update
  90.7 0.0 all-reduce.10.cloned.1.call-start
  90.7 0.0 copy-done.5
  90.7 0.6 dynamic-slice
  92.0 0.0 copy-done.3
  92.0 0.3 dynamic-update-slice
  92.3 22.1 %all-reduce = bf16[2304]{0:T(1024)(128)(2,1)S(1)} all-reduce(bf16[2304]{0:T(1024)(128)(2,1)S(1)} %dynamic-update-slice), channel_id=2, replica_groups=mesh['layer'=2,'latent'=8,'tok'=2] {'latent'}, use_global_device_ids=true, to_apply=%add | all-reduce | flops 2304 | bytes 9216
  114.4 0.0 copy-start.2
  114.4 53.9 %all-reduce.8.cloned.1.call-done = bf16[192,2304]{1,0:T(8,128)(2,1)} async-done(((bf16[192,2304]{1,0:T(8,128)(2,1)}), bf16[192,2304]{1,0:T(8,128)(2,1)}) %all-reduce.8.cloned.1.call-update) | async-done | bytes 884752 | tf_op jit(solution)/shard_map/psum | solution.py:23
  168.3 0.0 copy-done.1
  168.3 2.4 %fusion.10 = bf16[192,256]{1,0:T(8,128)(2,1)} fusion(bf16[1,256,2304]{2,1,0:T(8,128)(2,1)S(1)} %copy-done, bf16[192,2304]{1,0:T(8,128)(2,1)} %all-reduce.8.cloned.1.call-done, bf16[1,192,2304]{2,1,0:T(8,128)(2,1)S(1)} %copy-done.1, f32[2304]{0:T(1024)S(1)} %convert_element_type.66), kind=kOutput, calls=%fused_computation.12 | convolution fusion | flops 229195776 | bytes 3056640 | tf_op jit(solution)/shard_map/dot_general | solution.py:32
  170.7 0.0 all-reduce.10.cloned.1.call-update
  170.7 0.0 reduce-scatter.4.cloned.1.call-start
  170.8 20.7 %all-reduce.10.cloned.1.call-done = bf16[192,256]{1,0:T(8,128)(2,1)} async-done(((bf16[192,256]{1,0:T(8,128)(2,1)}), bf16[192,256]{1,0:T(8,128)(2,1)}) %all-reduce.10.cloned.1.call-update) | async-done | bytes 98320 | tf_op jit(solution)/shard_map/psum | solution.py:37
  191.4 0.0 copy-done.2
  191.4 1.4 fusion
  192.9 1.4 copy.11
  194.3 0.0 reduce-scatter.4.cloned.1.call-update
  194.3 0.0 all-reduce.12.cloned.1.call-start
  194.4 2.9 %fusion.1 = bf16[1,256,2304]{2,1,0:T(8,128)(2,1)} fusion(bf16[192,2304]{1,0:T(8,128)(2,1)} %all-reduce.8.cloned.1.call-done, bf16[1,192,2304]{2,1,0:T(8,128)(2,1)S(1)} %copy-done.1, f32[2304]{0:T(1024)S(1)} %convert_element_type.66, bf16[192,256]{1,0:T(8,128)(2,1)S(1)} %copy-done.2, f32[256]{0:T(256)S(1)} %copy-done.4), kind=kOutput, calls=%fused_computation.4 | convolution fusion | flops 230277120 | bytes 3057664 | tf_op jit(solution)/shard_map/dot_general | solution.py:29
  197.3 0.0 all-reduce.12.cloned.1.call-update
  197.3 5.7 %reduce-scatter.4.cloned.1.call-done = bf16[1152,256]{1,0:T(8,128)(2,1)} async-done(((bf16[2304,256]{1,0:T(8,128)(2,1)}), bf16[1152,256]{1,0:T(8,128)(2,1)}) %reduce-scatter.4.cloned.1.call-update) | async-done | bytes 589840
  203.0 1.4 copy.12
  204.4 1.1 copy.10
  205.4 20.7 %all-reduce.12.cloned.1.call-done = bf16[1,256,2304]{2,1,0:T(8,128)(2,1)} async-done(((bf16[1,256,2304]{2,1,0:T(8,128)(2,1)}), bf16[1,256,2304]{2,1,0:T(8,128)(2,1)}) %all-reduce.12.cloned.1.call-update) | async-done | bytes 1179664 | tf_op jit(solution)/shard_map/psum | solution.py:39
  226.2 2.4 %copy.18 = bf16[1,256,2304]{2,1,0:T(8,128)(2,1)} copy(bf16[1,256,2304]{2,1,0:T(8,128)(2,1)} %all-reduce.12.cloned.1.call-done) | data formatting | bytes 2359296
  (3 shorter events, 0.0 us)
Async XLA Ops:
  7.2 81.2 %copy-start = (bf16[1,256,2304]{2,1,0:T(8,128)(2,1)S(1)}, bf16[1,256,2304]{2,1,0:T(8,128)(2,1)}, u32[]{:S(2)}) copy-start(bf16[1,256,2304]{2,1,0:T(8,128)(2,1)} %param.8) | copy-start | bytes 3538948
  7.2 81.2 %all-reduce.6.cloned.1.call-start = ((), (), s32[]{:S(2)}) async-start(), calls=%async_computation.1 | async-start | bytes 196608 | tf_op jit(solution)/shard_map/psum | solution.py:20
  65.7 22.7 %copy-start.4 = (f32[256]{0:T(256)S(1)}, f32[256]{0:T(256)}, u32[]{:S(2)}) copy-start(f32[256]{0:T(256)} %param.7) | copy-start | bytes 3076
  68.3 22.5 %copy-start.5 = (u32[32]{0:T(128)S(1)}, u32[32]{0:T(128)}, u32[]{:S(2)}) copy-start(u32[32]{0:T(128)} %constant.17) | copy-start | bytes 388
  68.3 23.7 %copy-start.3 = (bf16[1,288]{1,0:T(2,128)(2,1)S(1)}, bf16[1,288]{1,0:T(2,128)(2,1)}, u32[]{:S(2)}) copy-start(bf16[1,288]{1,0:T(2,128)(2,1)} %param.9) | copy-start | bytes 1732
  68.3 100.0 %copy-start.1 = (bf16[1,192,2304]{2,1,0:T(8,128)(2,1)S(1)}, bf16[1,192,2304]{2,1,0:T(8,128)(2,1)}, u32[]{:S(2)}) copy-start(bf16[1,192,2304]{2,1,0:T(8,128)(2,1)} %copy.9) | copy-start | bytes 2654212
  68.3 100.0 %all-reduce.8.cloned.1.call-start = ((), (), s32[]{:S(2)}) async-start(), calls=%async_computation.2 | async-start | bytes 1769472 | tf_op jit(solution)/shard_map/psum | solution.py:23
  90.7 100.7 %all-reduce.10.cloned.1.call-start = ((), (), s32[]{:S(2)}) async-start(), calls=%async_computation.3 | async-start | bytes 196608 | tf_op jit(solution)/shard_map/psum | solution.py:37
  114.4 77.0 %copy-start.2 = (bf16[192,256]{1,0:T(8,128)(2,1)S(1)}, bf16[192,256]{1,0:T(8,128)(2,1)}, u32[]{:S(2)}) copy-start(bf16[192,256]{1,0:T(8,128)(2,1)} %all-reduce.6.cloned.1.call-done) | copy-start | bytes 294916
  170.7 32.3 %reduce-scatter.4.cloned.1.call-start = ((), (), s32[]{:S(2)}) async-start(), calls=%async_computation.5 | async-start | bytes 1769472
  194.3 31.8 %all-reduce.12.cloned.1.call-start = ((), (), s32[]{:S(2)}) async-start(), calls=%async_computation.4 | async-start | bytes 2359296 | tf_op jit(solution)/shard_map/psum | solution.py:39
Sparse Core Ops, SparseCore 0:
  68.4 19.8 all-reduce.5
  91.8 76.4 all-reduce.7
  171.1 20.2 all-reduce.9
  194.4 8.5 reduce-scatter.3
  205.2 20.9 all-reduce.11
where the time goes:
time: 235 us
  waiting for transfers between devices  121 us (51%)
  blocking collectives  73.7 us (31%)
  between operations  14.5 us (6%)
  local copies, waits for them, and re-layouts  13.9 us (6%)
  matrix products  11.6 us (5%)
    psum x1, waiting for transfers between devices, shards(): lax.psum(jnp.dot(act, decoder, preferred_element_type=jnp.float32).astype...  53.9 us
    all_gather x1, blocking collectives, shards(): lax.all_gather(resid, 'latent', axis=2, tiled=True)  51.7 us
    unnamed x1, blocking collectives  22.1 us
    psum x1, waiting for transfers between devices, shards(): grad_w_dec = lax.psum(dec_sum.astype(jnp.bfloat16), 'tok')  20.7 us
    psum x1, waiting for transfers between devices, shards(): lax.psum(act_grad.astype(jnp.bfloat16), 'layer').astype(jnp.float32)  20.7 us
    psum x1, waiting for transfers between devices, shards(): lax.psum(partial_value.astype(jnp.bfloat16), 'layer').astype(jnp.float32)  20 us
    unnamed x20, local copies, waits for them, and re-layouts  8.98 us
    unnamed x6, waiting for transfers between devices  5.8 us
  transfers between devices with their start and end apart: 5, of which 5 were waited for; matrix products, arithmetic and copies ran while one was open for 3% of the time, Pallas kernels for 0%

commit v1 on v0

--- a/solution.py
+++ b/solution.py
@@ -20,8 +20,11 @@
     pre = lax.psum(partial_value.astype(jnp.bfloat16), "layer").astype(jnp.float32) + b_enc
     act = (jax.nn.softplus(BETA * pre) / BETA).astype(jnp.bfloat16)
     slope = jax.nn.sigmoid(BETA * pre)
-    recon = lax.psum(
-        jnp.dot(act, decoder, preferred_element_type=jnp.float32).astype(jnp.bfloat16), "latent"
+    recon = jnp.sum(
+        lax.all_gather(
+            jnp.dot(act, decoder, preferred_element_type=jnp.float32).astype(jnp.bfloat16), "latent"
+        ),
+        axis=0,
     ).astype(jnp.float32)
     grad_all = (2.0 / tokens * (recon + bias_full - x_full.astype(jnp.float32))).astype(
         jnp.bfloat16

time: 235 us -> 269 us (1.14)
  waiting for transfers between devices: 121 us -> 150 us
  other arithmetic: 0.03 us -> 4.53 us
    all_gather x0 -> x1, waiting for transfers between devices: none -> 84.5 us  [shards(): lax.all_gather(jnp.dot(act, decoder, preferred_element_type=jnp.float32)....]
    psum x1 -> x0, waiting for transfers between devices: 53.9 us -> none  [shards(): lax.psum(jnp.dot(act, decoder, preferred_element_type=jnp.float32).astype...]
    reduce_sum x0 -> x1, other arithmetic: none -> 4.5 us  [shards(): jnp.sum(lax.all_gather(jnp.dot(act, decoder, preferred_element_type=jnp.f...]
    unnamed x20 -> x22, local copies, waits for them, and re-layouts: 8.98 us -> 8.99 us
  transfers between devices with their start and end apart: 5 -> 5, of which waited for: 5 -> 5; matrix products, arithmetic and copies ran while one was open for 3% -> 2% of each run, Pallas kernels for 0% -> 0%
where the time goes in v1:
time: 269 us; the launch traced here: 268 us
  waiting for transfers between devices  150 us (56%)
  blocking collectives  74.2 us (28%)
  between operations  14.5 us (5%)
  local copies, waits for them, and re-layouts  13.9 us (5%)
  matrix products  10.4 us (4%)
  other arithmetic  4.53 us (2%)
    all_gather x1, waiting for transfers between devices, shards(): lax.all_gather(jnp.dot(act, decoder, preferred_element_type=jnp.float32)....  84.5 us
    all_gather x1, blocking collectives, shards(): lax.all_gather(resid, 'latent', axis=2, tiled=True)  51.7 us
    unnamed x1, blocking collectives  22.6 us
    psum x1, waiting for transfers between devices, shards(): grad_w_dec = lax.psum(dec_sum.astype(jnp.bfloat16), 'tok')  20.7 us
    psum x1, waiting for transfers between devices, shards(): lax.psum(partial_value.astype(jnp.bfloat16), 'layer').astype(jnp.float32)  20 us
    psum x1, waiting for transfers between devices, shards(): lax.psum(act_grad.astype(jnp.bfloat16), 'layer').astype(jnp.float32)  19.5 us
    unnamed x22, local copies, waits for them, and re-layouts  8.99 us
    unnamed x6, waiting for transfers between devices  5.8 us
  transfers between devices with their start and end apart: 5, of which 5 were waited for; matrix products, arithmetic and copies ran while one was open for 2% of the time, Pallas kernels for 0%

profile of v1, /device:TPU:0, one launch (start us, length us, event | category | flops | bytes accessed | tf_op | source)
XLA Modules:
  0.0 268.3 jit_solution(11278597014392750402)
XLA Ops:
  7.2 0.0 copy-start
  7.2 0.0 all-reduce.5.cloned.1.call-start
  7.2 1.9 copy.10
  9.1 51.7 %all_gather.12 = bf16[1,192,2304]{1,0,2:T(2,128)(2,1)S(1)} all-gather(bf16[1,192,288]{1,0,2:T(2,128)(2,1)} %copy.10), channel_id=1, replica_groups=mesh['layer'=2,'latent'=8,'tok'=2] {'latent'}, dimensions={2}, use_global_device_ids=true | all-gather | bytes 995328 | tf_op jit(solution)/shard_map/all_gather | solution.py:12
  60.8 4.9 %copy.11 = bf16[1,192,2304]{2,1,0:T(8,128)(2,1)} copy(bf16[1,192,2304]{1,0,2:T(2,128)(2,1)S(1)} %all_gather.12) | data formatting | bytes 1769472 | tf_op jit(solution)/shard_map/all_gather | solution.py:12
  65.7 0.0 copy-start.5
  65.7 2.6 fusion.14
  68.3 0.0 copy-start.6
  68.3 0.0 copy-start.4
  68.3 0.0 all-reduce.5.cloned.1.call-update
  68.3 0.0 all-gather.4.cloned.1.call-start
  68.4 20.0 %all-reduce.5.cloned.1.call-done = bf16[192,256]{1,0:T(8,128)(2,1)} async-done(((bf16[192,256]{1,0:T(8,128)(2,1)}), bf16[192,256]{1,0:T(8,128)(2,1)}) %all-reduce.5.cloned.1.call-update) | async-done | bytes 98320 | tf_op jit(solution)/shard_map/psum | solution.py:20
  88.3 0.0 copy-done
  88.3 0.0 copy-done.5
  88.3 2.3 convolution_convert_fusion.2
  90.7 0.0 all-gather.4.cloned.1.call-update
  90.7 0.0 all-reduce.7.cloned.1.call-start
  90.7 0.0 copy-done.6
  90.7 0.6 dynamic-slice
  92.0 0.0 copy-done.4
  92.0 0.3 dynamic-update-slice
  92.3 22.6 %all-reduce = bf16[2304]{0:T(1024)(128)(2,1)S(1)} all-reduce(bf16[2304]{0:T(1024)(128)(2,1)S(1)} %dynamic-update-slice), channel_id=3, replica_groups=mesh['layer'=2,'latent'=8,'tok'=2] {'latent'}, use_global_device_ids=true, to_apply=%add | all-reduce | flops 2304 | bytes 9216
  114.9 84.5 %all-gather.4.cloned.1.call-done = bf16[1536,2304]{1,0:T(8,128)(2,1)} async-done(((bf16[192,2304]{1,0:T(8,128)(2,1)}), bf16[1536,2304]{1,0:T(8,128)(2,1)}) %all-gather.4.cloned.1.call-update) | async-done | bytes 7077904 | tf_op jit(solution)/shard_map/all_gather | solution.py:24
  199.4 0.0 copy-start.1
  199.4 4.5 %reduce_sum.12 = bf16[192,2304]{1,0:T(8,128)(2,1)S(1)} reduce(bf16[8,192,2304]{2,1,0:T(8,128)(2,1)} %bitcast.45, bf16[]{:T(256)} %constant.11.clone.1), dimensions={0}, to_apply=%region_1.2 | reduce | flops 3096576 | bytes 7962626 | tf_op jit(solution)/shard_map/reduce_sum | solution.py:23
  203.9 0.0 copy-done.1
  203.9 0.0 copy-start.2
  203.9 0.0 copy-start.3
  203.9 1.2 fusion.17
  205.1 0.0 copy-done.2
  205.1 0.0 all-reduce.7.cloned.1.call-update
  205.1 0.0 reduce-scatter.4.cloned.1.call-start
  205.2 19.5 %all-reduce.7.cloned.1.call-done = bf16[192,256]{1,0:T(8,128)(2,1)} async-done(((bf16[192,256]{1,0:T(8,128)(2,1)}), bf16[192,256]{1,0:T(8,128)(2,1)}) %all-reduce.7.cloned.1.call-update) | async-done | bytes 98320 | tf_op jit(solution)/shard_map/psum | solution.py:40
  224.7 0.0 copy-done.3
  224.7 1.4 fusion
  226.1 1.4 copy.14
  227.5 0.0 reduce-scatter.4.cloned.1.call-update
  227.5 0.0 all-reduce.9.cloned.1.call-start
  227.6 2.9 %fusion.1 = bf16[1,256,2304]{2,1,0:T(8,128)(2,1)} fusion(bf16[192,2304]{1,0:T(8,128)(2,1)} %copy-done.2, bf16[1,192,2304]{2,1,0:T(8,128)(2,1)S(1)} %copy-done.1, f32[2304]{0:T(1024)S(1)} %convert_element_type.94, bf16[192,256]{1,0:T(8,128)(2,1)S(1)} %copy-done.3, f32[256]{0:T(256)S(1)} %copy-done.5), kind=kOutput, calls=%fused_computation.4 | convolution fusion | flops 230277120 | bytes 3057664 | tf_op jit(solution)/shard_map/dot_general | solution.py:32
  230.5 0.0 all-reduce.9.cloned.1.call-update
  230.5 5.7 %reduce-scatter.4.cloned.1.call-done = bf16[1152,256]{1,0:T(8,128)(2,1)} async-done(((bf16[2304,256]{1,0:T(8,128)(2,1)}), bf16[1152,256]{1,0:T(8,128)(2,1)}) %reduce-scatter.4.cloned.1.call-update) | async-done | bytes 589840
  236.2 1.4 copy.15
  237.6 1.1 copy.13
  238.6 20.7 %all-reduce.9.cloned.1.call-done = bf16[1,256,2304]{2,1,0:T(8,128)(2,1)} async-done(((bf16[1,256,2304]{2,1,0:T(8,128)(2,1)}), bf16[1,256,2304]{2,1,0:T(8,128)(2,1)}) %all-reduce.9.cloned.1.call-update) | async-done | bytes 1179664 | tf_op jit(solution)/shard_map/psum | solution.py:42
  259.4 2.4 copy.20
  (3 shorter events, 0.0 us)
Async XLA Ops:
  7.2 81.2 %copy-start = (bf16[1,256,2304]{2,1,0:T(8,128)(2,1)S(1)}, bf16[1,256,2304]{2,1,0:T(8,128)(2,1)}, u32[]{:S(2)}) copy-start(bf16[1,256,2304]{2,1,0:T(8,128)(2,1)} %param.8) | copy-start | bytes 3538948
  7.2 81.2 %all-reduce.5.cloned.1.call-start = ((), (), s32[]{:S(2)}) async-start(), calls=%async_computation.1 | async-start | bytes 196608 | tf_op jit(solution)/shard_map/psum | solution.py:20
  65.7 22.7 %copy-start.5 = (f32[256]{0:T(256)S(1)}, f32[256]{0:T(256)}, u32[]{:S(2)}) copy-start(f32[256]{0:T(256)} %param.7) | copy-start | bytes 3076
  68.3 22.5 %copy-start.6 = (u32[32]{0:T(128)S(1)}, u32[32]{0:T(128)}, u32[]{:S(2)}) copy-start(u32[32]{0:T(128)} %constant.20) | copy-start | bytes 388
  68.3 23.7 %copy-start.4 = (bf16[1,288]{1,0:T(2,128)(2,1)S(1)}, bf16[1,288]{1,0:T(2,128)(2,1)}, u32[]{:S(2)}) copy-start(bf16[1,288]{1,0:T(2,128)(2,1)} %param.9) | copy-start | bytes 1732
  68.3 131.1 %all-gather.4.cloned.1.call-start = ((), (), s32[]{:S(2)}) async-start(), calls=%async_computation.4 | async-start | bytes 7962624 | tf_op jit(solution)/shard_map/all_gather | solution.py:24
  90.7 134.0 %all-reduce.7.cloned.1.call-start = ((), (), s32[]{:S(2)}) async-start(), calls=%async_computation.2 | async-start | bytes 196608 | tf_op jit(solution)/shard_map/psum | solution.py:40
  199.4 4.5 %copy-start.1 = (bf16[1,192,2304]{2,1,0:T(8,128)(2,1)S(1)}, bf16[1,192,2304]{2,1,0:T(8,128)(2,1)}, u32[]{:S(2)}) copy-start(bf16[1,192,2304]{2,1,0:T(8,128)(2,1)} %copy.11) | copy-start | bytes 2654212
  203.9 1.2 copy-start.2
  203.9 20.8 %copy-start.3 = (bf16[192,256]{1,0:T(8,128)(2,1)S(1)}, bf16[192,256]{1,0:T(8,128)(2,1)}, u32[]{:S(2)}) copy-start(bf16[192,256]{1,0:T(8,128)(2,1)} %all-reduce.5.cloned.1.call-done) | copy-start | bytes 294916
  205.1 31.1 %reduce-scatter.4.cloned.1.call-start = ((), (), s32[]{:S(2)}) async-start(), calls=%async_computation.5 | async-start | bytes 1769472
  227.5 31.8 %all-reduce.9.cloned.1.call-start = ((), (), s32[]{:S(2)}) async-start(), calls=%async_computation.3 | async-start | bytes 2359296 | tf_op jit(solution)/shard_map/psum | solution.py:42
Sparse Core Ops, SparseCore 0:
  68.4 19.8 all-reduce.4
  90.8 108.5 all-gather.3
  205.2 19.3 all-reduce.6
  227.7 8.5 reduce-scatter.3
  238.4 20.9 all-reduce.8
